TPU v7x, 32 devices: a whole 2x2x4 slice. The times are simulated.
32 devices in a mesh: rep: 8 (over y, x, core), shard: 4 (over z).
Axes of the slice: x: 2, y: 2, z: 4, core: 2. Of those that a mesh axis runs over, the one named last changes fastest.
Arguments:
- char_ids: int32 [128, 48], P(('rep', 'shard')), may hold values from 0 to 274
- prefix: int32 [128], P(('rep', 'shard')), may hold values from 4 to 24, as said below
- embedding: bfloat16 [2, 275, 100], replicated, may hold values from -6 to 6
- w_in: bfloat16 [2, 4, 100, 2048], P(None, None, None, 'shard'), may hold values from -0.625 to 0.625
- w_rec: bfloat16 [2, 4, 2048, 2048], P(None, None, None, 'shard'), may hold values from -0.125 to 0.125
- gate_bias: bfloat16 [2, 4, 2048], P(None, None, 'shard'), may hold values from -3 to 4
- w_out: bfloat16 [2, 2048, 275], P(None, 'shard'), may hold values from -0.875 to 0.875
- b_out: bfloat16 [2, 275], replicated, may hold values from -3 to 3
Outputs:
- grad_embed: float32 [2, 275, 100], replicated
- grad_in: float32 [2, 4, 100, 2048], P(None, None, None, 'shard')
- grad_rec: float32 [2, 4, 2048, 2048], P(None, None, 'rep', 'shard')
- grad_bias: float32 [2, 4, 2048], P(None, None, 'shard')
- grad_out: float32 [2, 2048, 275], P(None, 'shard')
- grad_bout: float32 [2, 275], replicated
Inputs may be any that keep to these rules, and one draw needn't show every extreme that they name: Some sequence has a prefix of exactly 24 characters.
All inputs are finite; a program needn't handle non-finite values.
Results may differ from a plain program's by a relative error of at most 0.0015.
Values may be sent and summed in bfloat16 or wider, within the bound.
A program may use at most 192 MiB of HBM per device.

v0:
```python
import math
import jax
import jax.numpy as jnp
from jax import lax
from jax.sharding import PartitionSpec as P

PRECISE = lax.Precision.HIGHEST


def one_hot(ids, width, out_type):
    return (ids[..., None] == jnp.arange(width, dtype=jnp.int32)).astype(out_type)


def loss_grad(logits, targets, active, factor):
    probabilities = jax.nn.softmax(logits, axis=-1)
    picked = one_hot(targets, logits.shape[-1], jnp.float32)
    return ((probabilities - picked) * (active * factor)[:, None]).astype(jnp.bfloat16)


def run_forward(projected, w_rec, start_pair, sender):

    def advance(state_pair, slot_proj):
        full_hidden, memory = state_pair
        gate_sum = slot_proj + jnp.einsum(
            "mbk,mgkn->mbgn", full_hidden, w_rec, preferred_element_type=jnp.float32
        )
        in_gate = jax.nn.sigmoid(gate_sum[..., 0, :])
        forget = jax.nn.sigmoid(gate_sum[..., 1, :])
        candidate = jnp.tanh(gate_sum[..., 2, :])
        out_gate = jax.nn.sigmoid(gate_sum[..., 3, :])
        new_memory = forget * memory + in_gate * candidate
        own_hidden = (out_gate * jnp.tanh(new_memory)).astype(jnp.bfloat16)
        new_full = sender(own_hidden)
        record = (
            jnp.stack([in_gate, forget, candidate, out_gate], axis=-2),
            new_memory,
            own_hidden,
            new_full,
        )
        return ((new_full, new_memory), record)

    return lax.scan(advance, start_pair, projected)


def run_backward(records, w_rec, start_pair, sender):

    def retreat(state_pair, record):
        from_later, cell_grad = state_pair
        gate_act, memory, prev_memory, from_decoder = record
        in_gate = gate_act[..., 0, :]
        forget = gate_act[..., 1, :]
        candidate = gate_act[..., 2, :]
        out_gate = gate_act[..., 3, :]
        grad_hidden = from_decoder + from_later
        squashed = jnp.tanh(memory)
        grad_memory = cell_grad + grad_hidden * out_gate * (1.0 - squashed * squashed)
        gate_grad = jnp.stack(
            [
                grad_memory * candidate * in_gate * (1.0 - in_gate),
                grad_memory * prev_memory * forget * (1.0 - forget),
                grad_memory * in_gate * (1.0 - candidate * candidate),
                grad_hidden * squashed * out_gate * (1.0 - out_gate),
            ],
            axis=-2,
        ).astype(jnp.bfloat16)
        partial_sum = jnp.einsum(
            "mbgn,mgkn->mbk", gate_grad, w_rec, preferred_element_type=jnp.float32
        )
        return ((sender(partial_sum), grad_memory * forget), gate_grad)

    return lax.scan(retreat, start_pair, records, reverse=True)


def shifted(values):
    return jnp.concatenate([jnp.zeros_like(values[:1]), values[:-1]], axis=0)


def shards(char_ids, prefix, embedding, w_in, w_rec, gate_bias, w_out, b_out):
    seq_dev, length = char_ids.shape
    half_len = length // 2
    vocab_size = embedding.shape[1]
    unit_count = w_rec.shape[2]
    shard_units = w_rec.shape[3]
    factor = 1.0 / math.sqrt(lax.axis_size("rep") * lax.axis_size("shard") * seq_dev * length)
    group_chars, group_prefix = (
        lax.all_gather(char_ids, "shard", axis=0, tiled=True),
        lax.all_gather(prefix, "shard", axis=0, tiled=True),
    )
    group_size = group_chars.shape[0]
    front_in = group_chars.T
    front_target = jnp.concatenate([group_chars[:, 1:], group_chars[:, :1]], axis=1).T
    timeline = jnp.arange(length, dtype=jnp.int32)[:, None]
    front_active = jnp.broadcast_to(
        (timeline < length - 1).astype(jnp.float32), (length, group_size)
    )
    reverse_steps = jnp.arange(half_len, dtype=jnp.int32)[:, None]
    back_in = jnp.take_along_axis(
        front_in, jnp.maximum(group_prefix[None, :] - 1 - reverse_steps, 0), axis=0
    )
    back_target = jnp.take_along_axis(
        front_in, jnp.maximum(group_prefix[None, :] - 2 - reverse_steps, 0), axis=0
    )
    back_active = (reverse_steps <= group_prefix[None, :] - 2).astype(jnp.float32)
    front_x = jnp.einsum(
        "tbv,ve->tbe",
        one_hot(front_in, vocab_size, jnp.bfloat16),
        embedding[0],
        preferred_element_type=jnp.float32,
    ).astype(jnp.bfloat16)
    back_x = jnp.einsum(
        "tbv,ve->tbe",
        one_hot(back_in, vocab_size, jnp.bfloat16),
        embedding[1],
        preferred_element_type=jnp.float32,
    ).astype(jnp.bfloat16)
    bias_wide = gate_bias.astype(jnp.float32)
    front_proj = (
        jnp.einsum("tbe,gen->tbgn", front_x, w_in[0], preferred_element_type=jnp.float32)
        + bias_wide[0]
    )
    back_proj = (
        jnp.einsum("tbe,gen->tbgn", back_x, w_in[1], preferred_element_type=jnp.float32)
        + bias_wide[1]
    )

    def move_both(own_hidden):
        return lax.all_gather(own_hidden, "shard", axis=2, tiled=True)

    def move_front(own_hidden):
        return lax.all_gather(own_hidden, "shard", axis=2, tiled=True)

    both_proj = jnp.stack([front_proj[:half_len], back_proj], axis=1)
    start_pair = (
        jnp.zeros((2, group_size, unit_count), jnp.bfloat16),
        jnp.zeros((2, group_size, shard_units), jnp.float32),
    )
    (mid_full, mid_memory), early_rec = run_forward(both_proj, w_rec, start_pair, move_both)
    front_weights = w_rec[:1]
    ignored, late_rec = run_forward(
        front_proj[half_len:, None], front_weights, (mid_full[:1], mid_memory[:1]), move_front
    )
    front_rec = tuple(
        (
            jnp.concatenate([head_part[:, :1], tail_part], axis=0)
            for head_part, tail_part in zip(early_rec, late_rec)
        )
    )
    back_rec = tuple((head_part[:, 1:] for head_part in early_rec))
    full_out = lax.all_gather(w_out, "shard", axis=1, tiled=True)
    first_seq = lax.axis_index("shard") * seq_dev
    front_rows = lax.dynamic_slice_in_dim(front_rec[3][:, 0], first_seq, seq_dev, axis=1).reshape(
        length * seq_dev, unit_count
    )
    back_rows = lax.dynamic_slice_in_dim(back_rec[3][:, 0], first_seq, seq_dev, axis=1).reshape(
        half_len * seq_dev, unit_count
    )
    own_front_target = lax.dynamic_slice_in_dim(front_target, first_seq, seq_dev, axis=1).reshape(
        -1
    )
    own_back_target = lax.dynamic_slice_in_dim(back_target, first_seq, seq_dev, axis=1).reshape(-1)
    own_front_active = lax.dynamic_slice_in_dim(front_active, first_seq, seq_dev, axis=1).reshape(
        -1
    )
    own_back_active = lax.dynamic_slice_in_dim(back_active, first_seq, seq_dev, axis=1).reshape(-1)
    front_logits = jnp.dot(front_rows, full_out[0], preferred_element_type=jnp.float32) + b_out[
        0
    ].astype(jnp.float32)
    back_logits = jnp.dot(back_rows, full_out[1], preferred_element_type=jnp.float32) + b_out[
        1
    ].astype(jnp.float32)
    front_grad = loss_grad(front_logits, own_front_target, own_front_active, factor)
    back_grad = loss_grad(back_logits, own_back_target, own_back_active, factor)
    front_part = jnp.einsum(
        "rv,kv->rk", front_grad, full_out[0], preferred_element_type=jnp.float32
    ).reshape(length, seq_dev, unit_count)
    back_part = jnp.einsum(
        "rv,kv->rk", back_grad, full_out[1], preferred_element_type=jnp.float32
    ).reshape(half_len, seq_dev, unit_count)
    front_dec, back_dec = (
        lax.all_to_all(front_part, "shard", split_axis=2, concat_axis=1, tiled=True),
        lax.all_to_all(back_part, "shard", split_axis=2, concat_axis=1, tiled=True),
    )
    front_dec = front_dec[:, None]
    back_dec = back_dec[:, None]
    out_whole = jnp.stack(
        [
            jnp.einsum("rk,rv->kv", front_rows, front_grad, preferred_element_type=jnp.float32),
            jnp.einsum("rk,rv->kv", back_rows, back_grad, preferred_element_type=jnp.float32),
        ]
    )
    out_grad = lax.psum_scatter(out_whole, "shard", scatter_dimension=1, tiled=True)
    bout_part = jnp.stack(
        [
            jnp.sum(front_grad, axis=0, dtype=jnp.float32),
            jnp.sum(back_grad, axis=0, dtype=jnp.float32),
        ]
    )

    def move_front_grad(partial_sum):
        return lax.psum_scatter(partial_sum, "shard", scatter_dimension=2, tiled=True)

    def move_both_grad(partial_sum):
        return lax.psum_scatter(partial_sum, "shard", scatter_dimension=2, tiled=True)

    front_prev_memory = shifted(front_rec[1])
    back_prev_memory = shifted(back_rec[1])
    blank_grad = jnp.zeros((1, group_size, shard_units), jnp.float32)
    late_records = (
        front_rec[0][half_len:],
        front_rec[1][half_len:],
        front_prev_memory[half_len:],
        front_dec[half_len:],
    )
    (carry_hidden, carry_memory), late_grads = run_backward(
        late_records, front_weights, (blank_grad, blank_grad), move_front_grad
    )
    prev_front = shifted(front_rec[3])[:, 0]
    prev_back = shifted(back_rec[3])[:, 0]
    early_records = (
        jnp.concatenate([front_rec[0][:half_len], back_rec[0]], axis=1),
        jnp.concatenate([front_rec[1][:half_len], back_rec[1]], axis=1),
        jnp.concatenate([front_prev_memory[:half_len], back_prev_memory], axis=1),
        jnp.concatenate([front_dec[:half_len], back_dec], axis=1),
    )
    start_back = (
        jnp.concatenate([carry_hidden, blank_grad], axis=0),
        jnp.concatenate([carry_memory, blank_grad], axis=0),
    )
    ignored, early_grads = run_backward(early_records, w_rec, start_back, move_both_grad)
    front_grads = jnp.concatenate([early_grads[:, :1], late_grads], axis=0)[:, 0]
    back_grads = early_grads[:, 1]
    front_rec_grad = jnp.einsum(
        "tbk,tbgn->gkn", prev_front, front_grads, preferred_element_type=jnp.float32
    )
    back_rec_grad = jnp.einsum(
        "tbk,tbgn->gkn", prev_back, back_grads, preferred_element_type=jnp.float32
    )
    rec_grad = lax.psum_scatter(
        jnp.stack([front_rec_grad, back_rec_grad]), "rep", scatter_dimension=2, tiled=True
    )
    in_grad = jnp.stack(
        [
            jnp.einsum("tbe,tbgn->gen", front_x, front_grads, preferred_element_type=jnp.float32),
            jnp.einsum("tbe,tbgn->gen", back_x, back_grads, preferred_element_type=jnp.float32),
        ]
    )
    bias_grad = jnp.stack(
        [
            jnp.sum(front_grads, axis=(0, 1), dtype=jnp.float32),
            jnp.sum(back_grads, axis=(0, 1), dtype=jnp.float32),
        ]
    )
    front_dx = jnp.einsum("tbgn,gen->tbe", front_grads, w_in[0], preferred_element_type=jnp.float32)
    back_dx = jnp.einsum("tbgn,gen->tbe", back_grads, w_in[1], preferred_element_type=jnp.float32)
    embed_grad = jnp.stack(
        [
            jnp.einsum(
                "tbv,tbe->ve",
                one_hot(front_in, vocab_size, jnp.float32),
                front_dx,
                precision=PRECISE,
            ),
            jnp.einsum(
                "tbv,tbe->ve", one_hot(back_in, vocab_size, jnp.float32), back_dx, precision=PRECISE
            ),
        ]
    )
    in_size = in_grad.size
    bias_size = bias_grad.size
    flat_grads = jnp.concatenate([in_grad.reshape(-1), bias_grad.reshape(-1), out_grad.reshape(-1)])
    summed_part = lax.psum_scatter(flat_grads, "rep", scatter_dimension=0, tiled=True)
    summed_flat = lax.all_gather(summed_part, "rep", axis=0, tiled=True)
    in_sum = summed_flat[:in_size].reshape(in_grad.shape)
    bias_sum = summed_flat[in_size : in_size + bias_size].reshape(bias_grad.shape)
    out_sum = summed_flat[in_size + bias_size :].reshape(out_grad.shape)
    embed_sum, bout_sum = lax.psum((embed_grad, bout_part), ("rep", "shard"))
    return (embed_sum, in_sum, rec_grad, bias_sum, out_sum, bout_sum)


def solution(mesh):
    in_specs = (
        P(("rep", "shard"), None),
        P(("rep", "shard")),
        P(),
        P(None, None, None, "shard"),
        P(None, None, None, "shard"),
        P(None, None, "shard"),
        P(None, "shard", None),
        P(),
    )
    out_specs = (
        P(),
        P(None, None, None, "shard"),
        P(None, None, "rep", "shard"),
        P(None, None, "shard"),
        P(None, "shard", None),
        P(),
    )
    return jax.shard_map(shards, mesh=mesh, in_specs=in_specs, out_specs=out_specs, check_vma=False)
```

profile of v0, /device:TPU:0, one launch (start us, length us, event | category | flops | bytes accessed | tf_op | source)
XLA Modules:
  0.0 3158.2 jit_solution(11104834085633158624)
XLA Ops:
  62.0 553.4 %while.76 = (s32[]{:T(128)}, bf16[2,16,2048]{2,1,0:T(8,128)(2,1)S(1)}, f32[2,16,512]{2,1,0:T(8,128)S(1)}, f32[24,2,16,4,512]{4,2,3,1,0:T(8,128)}, f32[24,2,16,51...) while((s32[]{:T(128)}, ...), condition=%wide.region_1.3_spmd.clone, body=%wide.region_0.2_spmd.clone.sunk | while | flops 269090816 | bytes 19464324 | solution.py:42
  616.6 474.4 %while.74 = (s32[]{:T(128)}, bf16[1,16,2048]{2,1,0:T(8,128)(2,1)S(1)}, f32[1,16,512]{2,1,0:T(8,128)S(1)}, f32[24,1,16,4,512]{4,2,3,1,0:T(8,128)}, f32[24,1,16,51...) while((s32[]{:T(128)}, ...), condition=%wide.region_3.5_spmd, body=%wide.region_2.4_spmd.sunk | while | flops 134537216 | bytes 9732213 | solution.py:42
  1205.7 637.4 %while.77 = (s32[]{:T(128)}, f32[1,16,512]{2,1,0:T(8,128)}, f32[1,16,512]{2,1,0:T(8,128)S(1)}, bf16[24,1,16,4,512]{4,2,3,1,0:T(8,128)(2,1)S(1)}, f32[24,1,16,512...) while((s32[]{:T(128)}, f32[1,16,512]{2,1,0:T(8,128)}, ...), condition=%wide.region_8.10_spmd.clone, body=%wide.region_6.9_spmd.clone.sunk | while | flops 134807552 | bytes 9961667 | solution.py:71
  1214.7 21.1 reduce-scatter.11.cloned.1.call-done
  1244.7 17.5 reduce-scatter.11.cloned.1.call-done
  1271.1 17.5 reduce-scatter.11.cloned.1.call-done
  1297.5 17.5 reduce-scatter.11.cloned.1.call-done
  1323.9 17.5 reduce-scatter.11.cloned.1.call-done
  1350.3 17.5 reduce-scatter.11.cloned.1.call-done
  1376.7 17.5 reduce-scatter.11.cloned.1.call-done
  1455.9 17.5 reduce-scatter.11.cloned.1.call-done
  1482.3 17.5 reduce-scatter.11.cloned.1.call-done
  1508.7 17.5 reduce-scatter.11.cloned.1.call-done
  1535.1 17.5 reduce-scatter.11.cloned.1.call-done
  1561.5 17.5 reduce-scatter.11.cloned.1.call-done
  1587.9 17.5 reduce-scatter.11.cloned.1.call-done
  1846.1 763.3 %while.75 = (s32[]{:T(128)}, f32[2,16,512]{2,1,0:T(8,128)}, f32[2,16,512]{2,1,0:T(8,128)S(1)}, bf16[24,2,16,4,512]{4,2,1,3,0:T(8,128)(2,1)S(1)}, f32[24,2,16,512...) while((s32[]{:T(128)}, f32[2,16,512]{2,1,0:T(8,128)}, ...), condition=%wide.region_13.15_spmd, body=%wide.region_11.14_spmd.sunk | while | flops 269598720 | bytes 19923120 | solution.py:71
  1860.0 18.0 reduce-scatter.9.cloned.1.call-done
  1891.7 18.0 reduce-scatter.9.cloned.1.call-done
  1923.5 18.0 reduce-scatter.9.cloned.1.call-done
  1955.3 18.0 reduce-scatter.9.cloned.1.call-done
  1987.1 18.0 reduce-scatter.9.cloned.1.call-done
  2018.9 18.0 reduce-scatter.9.cloned.1.call-done
  2050.7 18.0 reduce-scatter.9.cloned.1.call-done
  2082.5 18.0 reduce-scatter.9.cloned.1.call-done
  2114.3 18.0 reduce-scatter.9.cloned.1.call-done
  2146.1 18.0 reduce-scatter.9.cloned.1.call-done
  2177.9 18.0 reduce-scatter.9.cloned.1.call-done
  2209.7 18.0 reduce-scatter.9.cloned.1.call-done
  2241.5 18.0 reduce-scatter.9.cloned.1.call-done
  2273.3 18.0 reduce-scatter.9.cloned.1.call-done
  2305.1 18.0 reduce-scatter.9.cloned.1.call-done
  2337.0 18.1 reduce-scatter.9.cloned.1.call-done
  2368.8 18.0 reduce-scatter.9.cloned.1.call-done
  2400.6 18.0 reduce-scatter.9.cloned.1.call-done
  2432.4 18.0 reduce-scatter.9.cloned.1.call-done
  2464.2 18.0 reduce-scatter.9.cloned.1.call-done
  2496.0 18.0 reduce-scatter.9.cloned.1.call-done
  2527.8 18.0 reduce-scatter.9.cloned.1.call-done
  2559.6 18.0 reduce-scatter.9.cloned.1.call-done
  2591.4 18.0 reduce-scatter.9.cloned.1.call-done
  2623.7 70.3 %reduce-scatter.5.cloned.1.call-done = f32[2,512,275]{1,2,0:T(8,128)} async-done(((f32[2,2048,275]{1,2,0:T(8,128)}), f32[2,512,275]{1,2,0:T(8,128)}) %reduce-scatter.5.cloned.1.call-update) | async-done | bytes 1126416 | tf_op jit(solution)/shard_map/reduce_scatter | solution.py:191
  2714.3 57.1 %all-reduce.13.cloned.1.call-done = f32[695296]{0:T(1024)} async-done(((f32[695296]{0:T(1024)}), f32[695296]{0:T(1024)}) %all-reduce.13.cloned.1.call-update) | async-done | bytes 2781200
  2791.5 19.1 pad_maximum_fusion
  2811.3 39.5 %psum.15 = f32[2,275]{1,0:T(2,128)} all-reduce(f32[2,275]{1,0:T(2,128)S(1)} %pad_maximum_fusion.7), channel_id=1, replica_groups=mesh['rep'=8,'shard'=4] {'rep','shard'}, use_global_device_ids=true, to_apply=%region_22.24 | all-reduce | flops 550 | bytes 4400 | tf_op jit(solution)/shard_map/psum | solution.py:276
  2850.8 52.2 %all-reduce.11.cloned.1.call-done = f32[2,275,100]{2,1,0:T(8,128)} async-done(((f32[2,275,100]{2,1,0:T(8,128)}), f32[2,275,100]{2,1,0:T(8,128)}) %all-reduce.11.cloned.1.call-update) | async-done | bytes 220016 | tf_op jit(solution)/shard_map/psum | solution.py:276
  2904.8 32.3 %all-gather.7.cloned.1.call-done = f32[8,1,86912]{2,1,0:T(1,128)} async-done(((f32[1,1,86912]{2,1,0:T(1,128)}), f32[8,1,86912]{2,1,0:T(1,128)}) %all-gather.7.cloned.1.call-update) | async-done | bytes 2781200 | tf_op jit(solution)/shard_map/all_gather | solution.py:272
  2947.7 198.2 %reduce-scatter.7.cloned.1.call-done = f32[2,4,256,512]{2,3,1,0:T(8,128)} async-done(((f32[2,4,2048,512]{2,3,1,0:T(8,128)}), f32[2,4,256,512]{2,3,1,0:T(8,128)}) %reduce-scatter.7.cloned.1.call-update) | async-done | bytes 4194320 | tf_op jit(solution)/shard_map/reduce_scatter | solution.py:238
  (940 shorter events, 2007.4 us)
Async XLA Ops:
  7.2 1101.7 %all-gather.5.cloned.1.call-start = ((), (), s32[]{:S(2)}) async-start(), calls=%async_computation.6 | async-start | bytes 2867200 | tf_op jit(solution)/shard_map/all_gather | solution.py:149
  1144.9 30.4 all-to-all-start
  1205.7 30.1 reduce-scatter.11.cloned.1.call-start
  1235.8 26.4 reduce-scatter.11.cloned.1.call-start
  1262.2 26.4 reduce-scatter.11.cloned.1.call-start
  1288.6 26.4 reduce-scatter.11.cloned.1.call-start
  1315.0 26.4 reduce-scatter.11.cloned.1.call-start
  1341.4 26.4 reduce-scatter.11.cloned.1.call-start
  1367.8 26.4 reduce-scatter.11.cloned.1.call-start
  1394.2 26.4 reduce-scatter.11.cloned.1.call-start
  1499.8 26.4 reduce-scatter.11.cloned.1.call-start
  1526.2 26.4 reduce-scatter.11.cloned.1.call-start
  1552.6 26.4 reduce-scatter.11.cloned.1.call-start
  1579.0 26.4 reduce-scatter.11.cloned.1.call-start
  1605.4 26.4 reduce-scatter.11.cloned.1.call-start
  1631.8 26.4 reduce-scatter.11.cloned.1.call-start
  1763.8 26.4 reduce-scatter.11.cloned.1.call-start
  1790.2 26.4 reduce-scatter.11.cloned.1.call-start
  1816.6 26.4 reduce-scatter.11.cloned.1.call-start
  1846.1 31.8 %reduce-scatter.9.cloned.1.call-start = ((), (), s32[]{:S(2)}) async-start(), calls=%async_computation.12 | async-start | bytes 327680 | tf_op jit(solution)/shard_map/while/body/eval_jaxpr/reduce_scatter | solution.py:203
  1877.9 31.8 %reduce-scatter.9.cloned.1.call-start = ((), (), s32[]{:S(2)}) async-start(), calls=%async_computation.12 | async-start | bytes 327680 | tf_op jit(solution)/shard_map/while/body/eval_jaxpr/reduce_scatter | solution.py:203
  1909.7 31.8 %reduce-scatter.9.cloned.1.call-start = ((), (), s32[]{:S(2)}) async-start(), calls=%async_computation.12 | async-start | bytes 327680 | tf_op jit(solution)/shard_map/while/body/eval_jaxpr/reduce_scatter | solution.py:203
  1941.5 31.8 %reduce-scatter.9.cloned.1.call-start = ((), (), s32[]{:S(2)}) async-start(), calls=%async_computation.12 | async-start | bytes 327680 | tf_op jit(solution)/shard_map/while/body/eval_jaxpr/reduce_scatter | solution.py:203
  1973.3 31.8 %reduce-scatter.9.cloned.1.call-start = ((), (), s32[]{:S(2)}) async-start(), calls=%async_computation.12 | async-start | bytes 327680 | tf_op jit(solution)/shard_map/while/body/eval_jaxpr/reduce_scatter | solution.py:203
  2005.1 31.8 %reduce-scatter.9.cloned.1.call-start = ((), (), s32[]{:S(2)}) async-start(), calls=%async_computation.12 | async-start | bytes 327680 | tf_op jit(solution)/shard_map/while/body/eval_jaxpr/reduce_scatter | solution.py:203
  2036.9 31.8 %reduce-scatter.9.cloned.1.call-start = ((), (), s32[]{:S(2)}) async-start(), calls=%async_computation.12 | async-start | bytes 327680 | tf_op jit(solution)/shard_map/while/body/eval_jaxpr/reduce_scatter | solution.py:203
  2068.7 31.8 %reduce-scatter.9.cloned.1.call-start = ((), (), s32[]{:S(2)}) async-start(), calls=%async_computation.12 | async-start | bytes 327680 | tf_op jit(solution)/shard_map/while/body/eval_jaxpr/reduce_scatter | solution.py:203
  2100.5 31.8 %reduce-scatter.9.cloned.1.call-start = ((), (), s32[]{:S(2)}) async-start(), calls=%async_computation.12 | async-start | bytes 327680 | tf_op jit(solution)/shard_map/while/body/eval_jaxpr/reduce_scatter | solution.py:203
  2132.3 31.8 %reduce-scatter.9.cloned.1.call-start = ((), (), s32[]{:S(2)}) async-start(), calls=%async_computation.12 | async-start | bytes 327680 | tf_op jit(solution)/shard_map/while/body/eval_jaxpr/reduce_scatter | solution.py:203
  2164.1 31.8 %reduce-scatter.9.cloned.1.call-start = ((), (), s32[]{:S(2)}) async-start(), calls=%async_computation.12 | async-start | bytes 327680 | tf_op jit(solution)/shard_map/while/body/eval_jaxpr/reduce_scatter | solution.py:203
  2195.9 31.8 %reduce-scatter.9.cloned.1.call-start = ((), (), s32[]{:S(2)}) async-start(), calls=%async_computation.12 | async-start | bytes 327680 | tf_op jit(solution)/shard_map/while/body/eval_jaxpr/reduce_scatter | solution.py:203
  2227.7 31.8 %reduce-scatter.9.cloned.1.call-start = ((), (), s32[]{:S(2)}) async-start(), calls=%async_computation.12 | async-start | bytes 327680 | tf_op jit(solution)/shard_map/while/body/eval_jaxpr/reduce_scatter | solution.py:203
  2259.6 31.8 %reduce-scatter.9.cloned.1.call-start = ((), (), s32[]{:S(2)}) async-start(), calls=%async_computation.12 | async-start | bytes 327680 | tf_op jit(solution)/shard_map/while/body/eval_jaxpr/reduce_scatter | solution.py:203
  2291.4 31.8 %reduce-scatter.9.cloned.1.call-start = ((), (), s32[]{:S(2)}) async-start(), calls=%async_computation.12 | async-start | bytes 327680 | tf_op jit(solution)/shard_map/while/body/eval_jaxpr/reduce_scatter | solution.py:203
  2323.2 31.8 %reduce-scatter.9.cloned.1.call-start = ((), (), s32[]{:S(2)}) async-start(), calls=%async_computation.12 | async-start | bytes 327680 | tf_op jit(solution)/shard_map/while/body/eval_jaxpr/reduce_scatter | solution.py:203
  2355.0 31.8 %reduce-scatter.9.cloned.1.call-start = ((), (), s32[]{:S(2)}) async-start(), calls=%async_computation.12 | async-start | bytes 327680 | tf_op jit(solution)/shard_map/while/body/eval_jaxpr/reduce_scatter | solution.py:203
  2386.8 31.8 %reduce-scatter.9.cloned.1.call-start = ((), (), s32[]{:S(2)}) async-start(), calls=%async_computation.12 | async-start | bytes 327680 | tf_op jit(solution)/shard_map/while/body/eval_jaxpr/reduce_scatter | solution.py:203
  2418.6 31.8 %reduce-scatter.9.cloned.1.call-start = ((), (), s32[]{:S(2)}) async-start(), calls=%async_computation.12 | async-start | bytes 327680 | tf_op jit(solution)/shard_map/while/body/eval_jaxpr/reduce_scatter | solution.py:203
  2450.4 31.8 %reduce-scatter.9.cloned.1.call-start = ((), (), s32[]{:S(2)}) async-start(), calls=%async_computation.12 | async-start | bytes 327680 | tf_op jit(solution)/shard_map/while/body/eval_jaxpr/reduce_scatter | solution.py:203
  2482.2 31.8 %reduce-scatter.9.cloned.1.call-start = ((), (), s32[]{:S(2)}) async-start(), calls=%async_computation.12 | async-start | bytes 327680 | tf_op jit(solution)/shard_map/while/body/eval_jaxpr/reduce_scatter | solution.py:203
  2514.0 31.8 %reduce-scatter.9.cloned.1.call-start = ((), (), s32[]{:S(2)}) async-start(), calls=%async_computation.12 | async-start | bytes 327680 | tf_op jit(solution)/shard_map/while/body/eval_jaxpr/reduce_scatter | solution.py:203
  2545.8 31.8 %reduce-scatter.9.cloned.1.call-start = ((), (), s32[]{:S(2)}) async-start(), calls=%async_computation.12 | async-start | bytes 327680 | tf_op jit(solution)/shard_map/while/body/eval_jaxpr/reduce_scatter | solution.py:203
  2577.6 31.8 %reduce-scatter.9.cloned.1.call-start = ((), (), s32[]{:S(2)}) async-start(), calls=%async_computation.12 | async-start | bytes 327680 | tf_op jit(solution)/shard_map/while/body/eval_jaxpr/reduce_scatter | solution.py:203
  2609.4 84.6 %reduce-scatter.5.cloned.1.call-start = ((), (), s32[]{:S(2)}) async-start(), calls=%async_computation.8 | async-start | bytes 5734400 | tf_op jit(solution)/shard_map/reduce_scatter | solution.py:191
  2610.2 161.2 %all-reduce.13.cloned.1.call-start = ((), (), s32[]{:S(2)}) async-start(), calls=%async_computation.11 | async-start | bytes 5562368
  2704.2 198.8 %all-reduce.11.cloned.1.call-start = ((), (), s32[]{:S(2)}) async-start(), calls=%async_computation.7 | async-start | bytes 573440 | tf_op jit(solution)/shard_map/psum | solution.py:276
  2710.2 226.8 %all-gather.7.cloned.1.call-start = ((), (), s32[]{:S(2)}) async-start(), calls=%async_computation.10 | async-start | bytes 3128832 | tf_op jit(solution)/shard_map/all_gather | solution.py:272
  2773.5 372.4 %reduce-scatter.7.cloned.1.call-start = ((), (), s32[]{:S(2)}) async-start(), calls=%async_computation.9 | async-start | bytes 37748736 | tf_op jit(solution)/shard_map/reduce_scatter | solution.py:238
  (45 other events, 1454.6 us)
Sparse Core Ops, SparseCore 0:
  9.6 52.1 all-gather.4
  1214.8 20.9 reduce-scatter.10
  1244.8 17.3 reduce-scatter.10
  1271.2 17.3 reduce-scatter.10
  1297.6 17.3 reduce-scatter.10
  1324.0 17.3 reduce-scatter.10
  1350.4 17.3 reduce-scatter.10
  1376.8 17.3 reduce-scatter.10
  1403.2 17.3 reduce-scatter.10
  1429.6 17.3 reduce-scatter.10
  1456.0 17.3 reduce-scatter.10
  1482.4 17.3 reduce-scatter.10
  1508.8 17.3 reduce-scatter.10
  1535.2 17.3 reduce-scatter.10
  1561.6 17.3 reduce-scatter.10
  1588.0 17.3 reduce-scatter.10
  1614.4 17.3 reduce-scatter.10
  1640.8 17.3 reduce-scatter.10
  1667.2 17.3 reduce-scatter.10
  1860.1 17.8 reduce-scatter.8
  1891.8 17.8 reduce-scatter.8
  1923.6 17.8 reduce-scatter.8
  1955.4 17.8 reduce-scatter.8
  1987.2 17.8 reduce-scatter.8
  2019.0 17.8 reduce-scatter.8
  2050.8 17.8 reduce-scatter.8
  2082.6 17.8 reduce-scatter.8
  2114.4 17.8 reduce-scatter.8
  2146.2 17.8 reduce-scatter.8
  2178.0 17.8 reduce-scatter.8
  2209.8 17.8 reduce-scatter.8
  2241.6 17.8 reduce-scatter.8
  2273.4 17.8 reduce-scatter.8
  2305.2 17.8 reduce-scatter.8
  2337.0 17.9 reduce-scatter.8
  2368.9 17.8 reduce-scatter.8
  2400.7 17.8 reduce-scatter.8
  2432.5 17.8 reduce-scatter.8
  2464.3 17.8 reduce-scatter.8
  2496.1 17.8 reduce-scatter.8
  2527.9 17.8 reduce-scatter.8
  2559.7 17.8 reduce-scatter.8
  2591.5 17.8 reduce-scatter.8
  2612.6 81.3 reduce-scatter.4
  2704.3 67.0 all-reduce.12
  2777.6 125.3 all-reduce.10
  2905.3 31.7 all-gather.6
  2940.6 205.2 reduce-scatter.6
  (6 shorter events, 103.9 us)
where the time goes:
time: 3180 us; the launch traced here: 3160 us
  waiting for transfers between devices  1270 us (40%)
  matrix products  753 us (24%)
  blocking collectives  700 us (22%)
  local copies, waits for them, and re-layouts  205 us (6%)
  other arithmetic  204 us (6%)
    reduce_scatter x24, waiting for transfers between devices, move_both_grad(): lax.psum_scatter(partial_sum, 'shard', scatter_dimension=2, tiled=True)  432 us
    reduce_scatter x24, waiting for transfers between devices, move_front_grad(): lax.psum_scatter(partial_sum, 'shard', scatter_dimension=2, tiled=True)  424 us
    dot_general x48, matrix products, retreat(): jnp.einsum('mbgn,mgkn->mbk', gate_grad, w_rec, preferred_element_type=jnp...  413 us
    all_gather x24, blocking collectives, move_both(): return lax.all_gather(own_hidden, 'shard', axis=2, tiled=True)  322 us
    all_gather x24, blocking collectives, move_front(): return lax.all_gather(own_hidden, 'shard', axis=2, tiled=True)  316 us
    dot_general x48, matrix products, advance(): jnp.einsum('mbk,mgkn->mbgn', full_hidden, w_rec, preferred_element_type=j...  303 us
    reduce_scatter x1, waiting for transfers between devices, shards(): lax.psum_scatter(jnp.stack([front_rec_grad, back_rec_grad]), 'rep', scatt...  198 us
    reduce_scatter x1, waiting for transfers between devices, shards(): lax.psum_scatter(out_whole, 'shard', scatter_dimension=1, tiled=True)  70.3 us
  transfers between devices with their start and end apart: 56, of which 53 were waited for; matrix products, arithmetic and copies ran while one was open for 17% of the time, Pallas kernels for 0%

commit v1 on v0

--- a/solution.py
+++ b/solution.py
@@ -5,6 +5,18 @@
 from jax.sharding import PartitionSpec as P
 
 PRECISE = lax.Precision.HIGHEST
+
+
+def doubled_up(value, axis, dim):
+    ways, here, hop = (lax.axis_size(axis), lax.axis_index(axis), value.shape[dim])
+    line, have = (value, 1)
+    while have < ways:
+        line = jnp.concatenate(
+            [line, lax.ppermute(line, axis, [(d, (d - have) % ways) for d in range(ways)])],
+            axis=dim,
+        )
+        have = 2 * have
+    return jnp.roll(line, here * hop, axis=dim)
 
 
 def one_hot(ids, width, out_type):
@@ -127,7 +139,7 @@
         return lax.all_gather(own_hidden, "shard", axis=2, tiled=True)
 
     def move_front(own_hidden):
-        return lax.all_gather(own_hidden, "shard", axis=2, tiled=True)
+        return doubled_up(own_hidden, "shard", 2)
 
     both_proj = jnp.stack([front_proj[:half_len], back_proj], axis=1)
     start_pair = (

time: 3180 us -> 3080 us (0.969)
  blocking collectives: 700 us -> 384 us
  waiting for transfers between devices: 1270 us -> 1390 us
  starting transfers between devices: 10.5 us -> 126 us
    all_gather x24 -> x0, blocking collectives: 316 us -> none  [move_front(): return lax.all_gather(own_hidden, 'shard', axis=2, tiled=True)]
    ppermute x0 -> x48, waiting for transfers between devices: none -> 118 us  [doubled_up(): lax.ppermute(line, axis, [(d, (d - have) % ways) for d in range(ways)])]
    ppermute x0 -> x48, starting transfers between devices: none -> 115 us  [doubled_up(): lax.ppermute(line, axis, [(d, (d - have) % ways) for d in range(ways)])]
  transfers between devices with their start and end apart: 56 -> 104, of which waited for: 53 -> 101; matrix products, arithmetic and copies ran while one was open for 17% -> 17% of each run, Pallas kernels for 0% -> 0%
where the time goes in v1:
time: 3080 us; the launch traced here: 3060 us
  waiting for transfers between devices  1390 us (45%)
  matrix products  752 us (24%)
  blocking collectives  384 us (12%)
  local copies, waits for them, and re-layouts  207 us (7%)
  other arithmetic  188 us (6%)
  starting transfers between devices  126 us (4%)
    reduce_scatter x24, waiting for transfers between devices, move_both_grad(): lax.psum_scatter(partial_sum, 'shard', scatter_dimension=2, tiled=True)  432 us
    reduce_scatter x24, waiting for transfers between devices, move_front_grad(): lax.psum_scatter(partial_sum, 'shard', scatter_dimension=2, tiled=True)  424 us
    dot_general x48, matrix products, retreat(): jnp.einsum('mbgn,mgkn->mbk', gate_grad, w_rec, preferred_element_type=jnp...  413 us
    all_gather x24, blocking collectives, move_both(): return lax.all_gather(own_hidden, 'shard', axis=2, tiled=True)  323 us
    dot_general x48, matrix products, advance(): jnp.einsum('mbk,mgkn->mbgn', full_hidden, w_rec, preferred_element_type=j...  303 us
    reduce_scatter x1, waiting for transfers between devices, shards(): lax.psum_scatter(jnp.stack([front_rec_grad, back_rec_grad]), 'rep', scatt...  198 us
    ppermute x48, waiting for transfers between devices, doubled_up(): lax.ppermute(line, axis, [(d, (d - have) % ways) for d in range(ways)])  118 us
    ppermute x48, starting transfers between devices, doubled_up(): lax.ppermute(line, axis, [(d, (d - have) % ways) for d in range(ways)])  115 us
  transfers between devices with their start and end apart: 104, of which 101 were waited for; matrix products, arithmetic and copies ran while one was open for 17% of the time, Pallas kernels for 0%

profile of v1, /device:TPU:0, one launch (start us, length us, event | category | flops | bytes accessed | tf_op | source)
XLA Modules:
  0.0 3063.8 jit_solution(11676688708307208961)
XLA Ops:
  50.9 554.0 %while.78 = (s32[]{:T(128)}, bf16[2,16,2048]{2,1,0:T(8,128)(2,1)S(1)}, f32[2,16,512]{2,1,0:T(8,128)S(1)}, f32[24,2,16,4,512]{4,2,3,1,0:T(8,128)}, f32[24,2,16,51...) while((s32[]{:T(128)}, ...), condition=%wide.region_1.3_spmd.clone, body=%wide.region_0.2_spmd.clone.sunk | while | flops 269090816 | bytes 19464324 | solution.py:54
  630.1 378.4 %while.76 = (s32[]{:T(128)}, bf16[1,16,2048]{2,1,0:T(8,128)(2,1)S(1)}, f32[1,16,512]{2,1,0:T(8,128)S(1)}, f32[24,1,16,4,512]{4,2,3,1,0:T(8,128)}, f32[24,1,16,51...) while((s32[]{:T(128)}, ...), condition=%wide.region_3.5_spmd, body=%wide.region_2.4_spmd.sunk | while | flops 134602752 | bytes 10224052 | solution.py:54
  1111.4 637.2 %while.79 = (s32[]{:T(128)}, f32[1,16,512]{2,1,0:T(8,128)}, f32[1,16,512]{2,1,0:T(8,128)S(1)}, bf16[24,1,16,4,512]{4,2,3,1,0:T(8,128)(2,1)S(1)}, f32[24,1,16,512...) while((s32[]{:T(128)}, f32[1,16,512]{2,1,0:T(8,128)}, ...), condition=%wide.region_8.10_spmd.clone, body=%wide.region_6.9_spmd.clone.sunk | while | flops 134807552 | bytes 9961667 | solution.py:83
  1120.5 20.9 reduce-scatter.11.cloned.1.call-done
  1203.0 17.5 reduce-scatter.11.cloned.1.call-done
  1229.4 17.5 reduce-scatter.11.cloned.1.call-done
  1255.8 17.5 reduce-scatter.11.cloned.1.call-done
  1282.2 17.5 reduce-scatter.11.cloned.1.call-done
  1308.6 17.5 reduce-scatter.11.cloned.1.call-done
  1335.1 17.5 reduce-scatter.11.cloned.1.call-done
  1361.5 17.5 reduce-scatter.11.cloned.1.call-done
  1440.7 17.5 reduce-scatter.11.cloned.1.call-done
  1467.1 17.5 reduce-scatter.11.cloned.1.call-done
  1493.5 17.5 reduce-scatter.11.cloned.1.call-done
  1519.9 17.5 reduce-scatter.11.cloned.1.call-done
  1546.3 17.5 reduce-scatter.11.cloned.1.call-done
  1751.7 763.4 %while.77 = (s32[]{:T(128)}, f32[2,16,512]{2,1,0:T(8,128)}, f32[2,16,512]{2,1,0:T(8,128)S(1)}, bf16[24,2,16,4,512]{4,2,1,3,0:T(8,128)(2,1)S(1)}, f32[24,2,16,512...) while((s32[]{:T(128)}, f32[2,16,512]{2,1,0:T(8,128)}, ...), condition=%wide.region_13.15_spmd, body=%wide.region_11.14_spmd.sunk | while | flops 269598720 | bytes 19923120 | solution.py:83
  1765.6 17.9 reduce-scatter.9.cloned.1.call-done
  1797.2 18.0 reduce-scatter.9.cloned.1.call-done
  1829.0 18.0 reduce-scatter.9.cloned.1.call-done
  1860.8 18.0 reduce-scatter.9.cloned.1.call-done
  1892.6 18.0 reduce-scatter.9.cloned.1.call-done
  1924.4 18.0 reduce-scatter.9.cloned.1.call-done
  1956.2 18.0 reduce-scatter.9.cloned.1.call-done
  1988.0 18.1 reduce-scatter.9.cloned.1.call-done
  2019.9 18.0 reduce-scatter.9.cloned.1.call-done
  2051.7 18.0 reduce-scatter.9.cloned.1.call-done
  2083.5 18.0 reduce-scatter.9.cloned.1.call-done
  2115.3 18.0 reduce-scatter.9.cloned.1.call-done
  2147.1 18.1 reduce-scatter.9.cloned.1.call-done
  2179.0 18.0 reduce-scatter.9.cloned.1.call-done
  2210.8 18.0 reduce-scatter.9.cloned.1.call-done
  2242.6 18.0 reduce-scatter.9.cloned.1.call-done
  2274.4 18.0 reduce-scatter.9.cloned.1.call-done
  2306.2 18.0 reduce-scatter.9.cloned.1.call-done
  2338.0 18.0 reduce-scatter.9.cloned.1.call-done
  2369.8 18.0 reduce-scatter.9.cloned.1.call-done
  2401.6 18.0 reduce-scatter.9.cloned.1.call-done
  2433.4 18.0 reduce-scatter.9.cloned.1.call-done
  2465.2 18.0 reduce-scatter.9.cloned.1.call-done
  2497.0 18.0 reduce-scatter.9.cloned.1.call-done
  2529.3 70.3 %reduce-scatter.5.cloned.1.call-done = f32[2,512,275]{1,2,0:T(8,128)} async-done(((f32[2,2048,275]{1,2,0:T(8,128)}), f32[2,512,275]{1,2,0:T(8,128)}) %reduce-scatter.5.cloned.1.call-update) | async-done | bytes 1126416 | tf_op jit(solution)/shard_map/reduce_scatter | solution.py:203
  2619.9 57.1 %all-reduce.13.cloned.1.call-done = f32[695296]{0:T(1024)} async-done(((f32[695296]{0:T(1024)}), f32[695296]{0:T(1024)}) %all-reduce.13.cloned.1.call-update) | async-done | bytes 2781200
  2697.2 19.1 pad_maximum_fusion.1
  2717.0 39.5 %psum.15 = f32[2,275]{1,0:T(2,128)} all-reduce(f32[2,275]{1,0:T(2,128)S(1)} %pad_maximum_fusion.8), channel_id=1, replica_groups=mesh['rep'=8,'shard'=4] {'rep','shard'}, use_global_device_ids=true, to_apply=%region_22.24 | all-reduce | flops 550 | bytes 4400 | tf_op jit(solution)/shard_map/psum | solution.py:288
  2756.5 52.1 %all-reduce.11.cloned.1.call-done = f32[2,275,100]{2,1,0:T(8,128)} async-done(((f32[2,275,100]{2,1,0:T(8,128)}), f32[2,275,100]{2,1,0:T(8,128)}) %all-reduce.11.cloned.1.call-update) | async-done | bytes 220016 | tf_op jit(solution)/shard_map/psum | solution.py:288
  2810.4 32.3 %all-gather.7.cloned.1.call-done = f32[8,1,86912]{2,1,0:T(1,128)} async-done(((f32[1,1,86912]{2,1,0:T(1,128)}), f32[8,1,86912]{2,1,0:T(1,128)}) %all-gather.7.cloned.1.call-update) | async-done | bytes 2781200 | tf_op jit(solution)/shard_map/all_gather | solution.py:284
  2853.3 198.2 %reduce-scatter.7.cloned.1.call-done = f32[2,4,256,512]{2,3,1,0:T(8,128)} async-done(((f32[2,4,2048,512]{2,3,1,0:T(8,128)}), f32[2,4,256,512]{2,3,1,0:T(8,128)}) %reduce-scatter.7.cloned.1.call-update) | async-done | bytes 4194320 | tf_op jit(solution)/shard_map/reduce_scatter | solution.py:250
  (1158 shorter events, 1912.2 us)
Async XLA Ops:
  7.2 1004.7 %all-gather.5.cloned.1.call-start = ((), (), s32[]{:S(2)}) async-start(), calls=%async_computation.6 | async-start | bytes 2867200 | tf_op jit(solution)/shard_map/all_gather | solution.py:161
  1050.6 30.4 all-to-all-start
  1111.5 29.9 reduce-scatter.11.cloned.1.call-start
  1167.7 26.4 reduce-scatter.11.cloned.1.call-start
  1194.1 26.4 reduce-scatter.11.cloned.1.call-start
  1220.5 26.4 reduce-scatter.11.cloned.1.call-start
  1246.9 26.4 reduce-scatter.11.cloned.1.call-start
  1273.3 26.4 reduce-scatter.11.cloned.1.call-start
  1299.8 26.4 reduce-scatter.11.cloned.1.call-start
  1326.2 26.4 reduce-scatter.11.cloned.1.call-start
  1352.6 26.4 reduce-scatter.11.cloned.1.call-start
  1379.0 26.4 reduce-scatter.11.cloned.1.call-start
  1405.4 26.4 reduce-scatter.11.cloned.1.call-start
  1484.6 26.4 reduce-scatter.11.cloned.1.call-start
  1511.0 26.4 reduce-scatter.11.cloned.1.call-start
  1537.4 26.4 reduce-scatter.11.cloned.1.call-start
  1563.8 26.4 reduce-scatter.11.cloned.1.call-start
  1590.2 26.4 reduce-scatter.11.cloned.1.call-start
  1616.6 26.4 reduce-scatter.11.cloned.1.call-start
  1751.7 31.8 %reduce-scatter.9.cloned.1.call-start = ((), (), s32[]{:S(2)}) async-start(), calls=%async_computation.12 | async-start | bytes 327680 | tf_op jit(solution)/shard_map/while/body/eval_jaxpr/reduce_scatter | solution.py:215
  1783.5 31.8 %reduce-scatter.9.cloned.1.call-start = ((), (), s32[]{:S(2)}) async-start(), calls=%async_computation.12 | async-start | bytes 327680 | tf_op jit(solution)/shard_map/while/body/eval_jaxpr/reduce_scatter | solution.py:215
  1815.2 31.8 %reduce-scatter.9.cloned.1.call-start = ((), (), s32[]{:S(2)}) async-start(), calls=%async_computation.12 | async-start | bytes 327680 | tf_op jit(solution)/shard_map/while/body/eval_jaxpr/reduce_scatter | solution.py:215
  1847.0 31.8 %reduce-scatter.9.cloned.1.call-start = ((), (), s32[]{:S(2)}) async-start(), calls=%async_computation.12 | async-start | bytes 327680 | tf_op jit(solution)/shard_map/while/body/eval_jaxpr/reduce_scatter | solution.py:215
  1878.8 31.8 %reduce-scatter.9.cloned.1.call-start = ((), (), s32[]{:S(2)}) async-start(), calls=%async_computation.12 | async-start | bytes 327680 | tf_op jit(solution)/shard_map/while/body/eval_jaxpr/reduce_scatter | solution.py:215
  1910.6 31.8 %reduce-scatter.9.cloned.1.call-start = ((), (), s32[]{:S(2)}) async-start(), calls=%async_computation.12 | async-start | bytes 327680 | tf_op jit(solution)/shard_map/while/body/eval_jaxpr/reduce_scatter | solution.py:215
  1942.4 31.8 %reduce-scatter.9.cloned.1.call-start = ((), (), s32[]{:S(2)}) async-start(), calls=%async_computation.12 | async-start | bytes 327680 | tf_op jit(solution)/shard_map/while/body/eval_jaxpr/reduce_scatter | solution.py:215
  1974.3 31.9 %reduce-scatter.9.cloned.1.call-start = ((), (), s32[]{:S(2)}) async-start(), calls=%async_computation.12 | async-start | bytes 327680 | tf_op jit(solution)/shard_map/while/body/eval_jaxpr/reduce_scatter | solution.py:215
  2006.1 31.8 %reduce-scatter.9.cloned.1.call-start = ((), (), s32[]{:S(2)}) async-start(), calls=%async_computation.12 | async-start | bytes 327680 | tf_op jit(solution)/shard_map/while/body/eval_jaxpr/reduce_scatter | solution.py:215
  2037.9 31.8 %reduce-scatter.9.cloned.1.call-start = ((), (), s32[]{:S(2)}) async-start(), calls=%async_computation.12 | async-start | bytes 327680 | tf_op jit(solution)/shard_map/while/body/eval_jaxpr/reduce_scatter | solution.py:215
  2069.7 31.8 %reduce-scatter.9.cloned.1.call-start = ((), (), s32[]{:S(2)}) async-start(), calls=%async_computation.12 | async-start | bytes 327680 | tf_op jit(solution)/shard_map/while/body/eval_jaxpr/reduce_scatter | solution.py:215
  2101.5 31.8 %reduce-scatter.9.cloned.1.call-start = ((), (), s32[]{:S(2)}) async-start(), calls=%async_computation.12 | async-start | bytes 327680 | tf_op jit(solution)/shard_map/while/body/eval_jaxpr/reduce_scatter | solution.py:215
  2133.3 31.8 %reduce-scatter.9.cloned.1.call-start = ((), (), s32[]{:S(2)}) async-start(), calls=%async_computation.12 | async-start | bytes 327680 | tf_op jit(solution)/shard_map/while/body/eval_jaxpr/reduce_scatter | solution.py:215
  2165.2 31.8 %reduce-scatter.9.cloned.1.call-start = ((), (), s32[]{:S(2)}) async-start(), calls=%async_computation.12 | async-start | bytes 327680 | tf_op jit(solution)/shard_map/while/body/eval_jaxpr/reduce_scatter | solution.py:215
  2197.0 31.8 %reduce-scatter.9.cloned.1.call-start = ((), (), s32[]{:S(2)}) async-start(), calls=%async_computation.12 | async-start | bytes 327680 | tf_op jit(solution)/shard_map/while/body/eval_jaxpr/reduce_scatter | solution.py:215
  2228.8 31.8 %reduce-scatter.9.cloned.1.call-start = ((), (), s32[]{:S(2)}) async-start(), calls=%async_computation.12 | async-start | bytes 327680 | tf_op jit(solution)/shard_map/while/body/eval_jaxpr/reduce_scatter | solution.py:215
  2260.6 31.8 %reduce-scatter.9.cloned.1.call-start = ((), (), s32[]{:S(2)}) async-start(), calls=%async_computation.12 | async-start | bytes 327680 | tf_op jit(solution)/shard_map/while/body/eval_jaxpr/reduce_scatter | solution.py:215
  2292.4 31.8 %reduce-scatter.9.cloned.1.call-start = ((), (), s32[]{:S(2)}) async-start(), calls=%async_computation.12 | async-start | bytes 327680 | tf_op jit(solution)/shard_map/while/body/eval_jaxpr/reduce_scatter | solution.py:215
  2324.2 31.8 %reduce-scatter.9.cloned.1.call-start = ((), (), s32[]{:S(2)}) async-start(), calls=%async_computation.12 | async-start | bytes 327680 | tf_op jit(solution)/shard_map/while/body/eval_jaxpr/reduce_scatter | solution.py:215
  2356.0 31.8 %reduce-scatter.9.cloned.1.call-start = ((), (), s32[]{:S(2)}) async-start(), calls=%async_computation.12 | async-start | bytes 327680 | tf_op jit(solution)/shard_map/while/body/eval_jaxpr/reduce_scatter | solution.py:215
  2387.8 31.8 %reduce-scatter.9.cloned.1.call-start = ((), (), s32[]{:S(2)}) async-start(), calls=%async_computation.12 | async-start | bytes 327680 | tf_op jit(solution)/shard_map/while/body/eval_jaxpr/reduce_scatter | solution.py:215
  2419.6 31.8 %reduce-scatter.9.cloned.1.call-start = ((), (), s32[]{:S(2)}) async-start(), calls=%async_computation.12 | async-start | bytes 327680 | tf_op jit(solution)/shard_map/while/body/eval_jaxpr/reduce_scatter | solution.py:215
  2451.4 31.8 %reduce-scatter.9.cloned.1.call-start = ((), (), s32[]{:S(2)}) async-start(), calls=%async_computation.12 | async-start | bytes 327680 | tf_op jit(solution)/shard_map/while/body/eval_jaxpr/reduce_scatter | solution.py:215
  2483.2 31.8 %reduce-scatter.9.cloned.1.call-start = ((), (), s32[]{:S(2)}) async-start(), calls=%async_computation.12 | async-start | bytes 327680 | tf_op jit(solution)/shard_map/while/body/eval_jaxpr/reduce_scatter | solution.py:215
  2515.1 84.6 %reduce-scatter.5.cloned.1.call-start = ((), (), s32[]{:S(2)}) async-start(), calls=%async_computation.8 | async-start | bytes 5734400 | tf_op jit(solution)/shard_map/reduce_scatter | solution.py:203
  2515.8 161.2 %all-reduce.13.cloned.1.call-start = ((), (), s32[]{:S(2)}) async-start(), calls=%async_computation.11 | async-start | bytes 5562368
  2609.8 198.8 %all-reduce.11.cloned.1.call-start = ((), (), s32[]{:S(2)}) async-start(), calls=%async_computation.7 | async-start | bytes 573440 | tf_op jit(solution)/shard_map/psum | solution.py:288
  2615.8 226.9 %all-gather.7.cloned.1.call-start = ((), (), s32[]{:S(2)}) async-start(), calls=%async_computation.10 | async-start | bytes 3128832 | tf_op jit(solution)/shard_map/all_gather | solution.py:284
  2679.1 372.4 %reduce-scatter.7.cloned.1.call-start = ((), (), s32[]{:S(2)}) async-start(), calls=%async_computation.9 | async-start | bytes 37748736 | tf_op jit(solution)/shard_map/reduce_scatter | solution.py:250
  (94 other events, 1264.7 us)
Sparse Core Ops, SparseCore 0:
  10.1 52.8 all-gather.4
  1120.6 20.7 reduce-scatter.10
  1176.7 17.3 reduce-scatter.10
  1203.1 17.3 reduce-scatter.10
  1229.5 17.3 reduce-scatter.10
  1255.9 17.3 reduce-scatter.10
  1282.3 17.3 reduce-scatter.10
  1308.8 17.3 reduce-scatter.10
  1335.2 17.3 reduce-scatter.10
  1361.6 17.3 reduce-scatter.10
  1388.0 17.3 reduce-scatter.10
  1414.4 17.3 reduce-scatter.10
  1440.8 17.3 reduce-scatter.10
  1467.2 17.3 reduce-scatter.10
  1493.6 17.3 reduce-scatter.10
  1520.0 17.3 reduce-scatter.10
  1546.4 17.3 reduce-scatter.10
  1572.8 17.3 reduce-scatter.10
  1599.2 17.3 reduce-scatter.10
  1765.6 17.7 reduce-scatter.8
  1797.3 17.8 reduce-scatter.8
  1829.1 17.8 reduce-scatter.8
  1860.9 17.8 reduce-scatter.8
  1892.7 17.8 reduce-scatter.8
  1924.5 17.8 reduce-scatter.8
  1956.3 17.8 reduce-scatter.8
  1988.1 17.9 reduce-scatter.8
  2020.0 17.8 reduce-scatter.8
  2051.8 17.8 reduce-scatter.8
  2083.6 17.8 reduce-scatter.8
  2115.4 17.8 reduce-scatter.8
  2147.2 17.9 reduce-scatter.8
  2179.1 17.8 reduce-scatter.8
  2210.9 17.8 reduce-scatter.8
  2242.7 17.8 reduce-scatter.8
  2274.5 17.8 reduce-scatter.8
  2306.3 17.8 reduce-scatter.8
  2338.1 17.8 reduce-scatter.8
  2369.9 17.8 reduce-scatter.8
  2401.7 17.8 reduce-scatter.8
  2433.5 17.8 reduce-scatter.8
  2465.3 17.8 reduce-scatter.8
  2497.1 17.8 reduce-scatter.8
  2518.2 81.3 reduce-scatter.4
  2609.9 67.0 all-reduce.12
  2683.2 125.3 all-reduce.10
  2810.9 31.7 all-gather.6
  2846.3 205.2 reduce-scatter.6
  (6 shorter events, 103.8 us)
